TPU v7x, 32 devices: a whole 2x2x4 slice. The times are simulated.
32 devices in a mesh: gx: 4 (over z), gy: 4 (over x, core), tracer: 2 (over y).
Axes of the slice: x: 2, y: 2, z: 4, core: 2. Of those that a mesh axis runs over, the one named last changes fastest.
Arguments:
- biology_concentration: float32 [24, 8, 256, 512], P('tracer', None, 'gy', 'gx'), may hold values from 0.1 to 2
- flow_vectors: float32 [2, 8, 256, 512], P(None, 'tracer', 'gy', 'gx'), may hold values from -0.25 to 0.25
- thermal_anomaly: float32 [8, 256, 512], P('tracer', 'gy', 'gx'), may hold values from -6 to 6
- diffusivity_profile: float32 [8, 256, 512], P(None, 'gy', 'gx'), may hold values from 0.02 to 0.24
- solar_flux_field: float32 [256, 512], P('gy', 'gx'), may hold values from 0.5 to 2
- ecosystem_coefficients: float32 [24], P('tracer'), may hold values from 0.05 to 0.5
- ocean_indicator: int32 [256, 512], P('gy', 'gx'), may hold values 0 or 1
- floor_tier_number: int32 [256, 512], P('gy', 'gx'), may hold values from 1 to 8
Outputs:
- tracers_out: float32 [24, 8, 256, 512], P('tracer', None, 'gy', 'gx')
- currents_out: float32 [2, 8, 256, 512], P(None, 'tracer', 'gy', 'gx')
- temperature_out: float32 [8, 256, 512], P('tracer', 'gy', 'gx')
All inputs are finite; a program needn't handle non-finite values. No bound on the sum of `ocean_indicator` on one device may be relied on, other than what follows from the above.
Results may differ from a plain program's by a relative error of at most 0.0003.
Values sent between devices are 32-bit elements; how exact they have to be, the bound alone decides.
A program may use at most 64 MiB of HBM per device.

v0:
```python
import functools

import jax
import jax.numpy as jnp
from jax import lax
from jax.experimental import pallas as pl
from jax.experimental.pallas import tpu as pltpu
from jax.sharding import PartitionSpec as P

STEPS = 2
viscosity = 0.2
water_absorb = 0.04
plankton_absorb = 0.03
heat_share = 0.5
light_half = 0.3
nutrient_half = 0.5
SLOTS = 32
F32 = jnp.float32


def minmod(a, b):
    return jnp.maximum(jnp.minimum(a, b), jnp.minimum(jnp.maximum(a, b), 0.0))


def kernel(nx, ny, nt, NT, LV, LO, H, W,
           c_ref, flow_ref, temp_ref, kv_ref, sol_ref, eco_ref, ocean_ref, floor_ref,
           out_ref, outf_ref, outt_ref,
           cp1, cp2, xp1, xp2, xe1, xe2, xw1, xw2, hc, hs,
           flow_all, temp_all, flow_out, coef, sy, part, arecv,
           fs, fr, hsend, hrecv, asend, arec_sem):
    gx, gy, t = lax.axis_index("gx"), lax.axis_index("gy"), lax.axis_index("tracer")
    WET, TF, UF, VF = 0, NT + 1, NT + 2, NT + 3
    G = H // SLOTS
    NCH = asend.shape[1]
    CH = H // NCH
    own = pl.multiple_of(t * (LO * H), 8)
    lane = lax.broadcasted_iota(jnp.int32, (LV, W), 1)
    level = lax.broadcasted_iota(jnp.int32, (LV, W), 0)
    lane_slot = lane // 4
    first, last = lane == 0, lane == W - 1
    half = (lane % 4) < 2
    sgn = jnp.where(half, 1.0, -1.0).astype(F32)

    has = (gy < ny - 1, gy > 0, gx < nx - 1, gx > 0)
    came = (gy > 0, gy < ny - 1, gx > 0, gx < nx - 1)
    peer = ({"gy": lax.rem(gy + 1, ny)}, {"gy": lax.rem(gy + ny - 1, ny)},
            {"gx": lax.rem(gx + 1, nx)}, {"gx": lax.rem(gx + nx - 1, nx)})
    barrier = pltpu.get_barrier_semaphore()
    for d in range(4):
        @pl.when(has[d])
        def _():
            pl.semaphore_signal(barrier, inc=1, device_id=peer[d], device_id_type=pl.DeviceIdType.MESH)
    for d in range(1, nt):
        pl.semaphore_signal(barrier, inc=1, device_id={"tracer": lax.rem(t + d, nt)},
                            device_id_type=pl.DeviceIdType.MESH)
    pl.semaphore_wait(barrier, sum(x.astype(jnp.int32) for x in has) + (nt - 1))

    def remote(src, dst, ss, rs, dev):
        return pltpu.make_async_remote_copy(src_ref=src, dst_ref=dst, send_sem=ss, recv_sem=rs,
                                            device_id=dev, device_id_type=pl.DeviceIdType.MESH)

    flows = [remote(flow_ref, flow_all.at[:, pl.ds(own, LO * H), :], fs.at[d], fr.at[d],
                    {"tracer": lax.rem(t + d, nt)}) for d in range(1, nt)]
    for cp in flows:
        cp.start()

    def exchange(step, grp, cp, xp, xe, xw, lo, n):
        f = pl.ds(lo, n)
        pairs = ((cp.at[f, pl.ds(H, 2)], cp.at[f, pl.ds(0, 2)]),
                 (cp.at[f, pl.ds(2, 2)], cp.at[f, pl.ds(H + 2, 2)]),
                 (xp.at[f], xw.at[f]), (xp.at[f], xe.at[f]))
        return [remote(s, r, hsend.at[step, grp, d], hrecv.at[step, grp, d], peer[d])
                for d, (s, r) in enumerate(pairs)]

    def start(copies, dirs):
        for d in dirs:
            @pl.when(has[d])
            def _():
                copies[d].start()

    def wait_recv(copies):
        for d in range(4):
            @pl.when(came[d])
            def _():
                copies[d].wait_recv()

    def wait_send(copies):
        for d in range(4):
            @pl.when(has[d])
            def _():
                copies[d].wait_send()

    def pack(cp, xp, lo, n):
        def body(f, _):
            for g in range(G):
                acc = jnp.zeros((LV, W), F32)
                for j in range(SLOTS):
                    row = cp[f, 2 + g * SLOTS + j]
                    acc = jnp.where(lane_slot == j, pltpu.roll(row, (4 * j + 2) % W, 1), acc)
                xp[f, g] = acc
            return 0
        lax.fori_loop(lo, lo + n, body, 0)

    def unpack(xp, xe, xw, lo, n):
        def body(f, _):
            for g in range(G):
                o, e, w = xp[f, g], xe[f, g], xw[f, g]
                near = jnp.where(half, pltpu.roll(e, W - 1, 1), pltpu.roll(w, 1, 1))
                far = jnp.where(half, pltpu.roll(e, W - 2, 1), pltpu.roll(w, 2, 1))
                hc[f, g] = near
                hs[f, g] = sgn * minmod(far - near, near - o)
            return 0
        lax.fori_loop(lo, lo + n, body, 0)

    def clear_edges(cp, xe, xw):
        NF = NT + 4
        zrow = jnp.zeros((NF, 2, LV, W), F32)
        zx = jnp.zeros((NF, G, LV, W), F32)
        @pl.when(gy == 0)
        def _():
            cp[:, 0:2] = zrow
        @pl.when(gy == ny - 1)
        def _():
            cp[:, H + 2:H + 4] = zrow
        @pl.when(gx == nx - 1)
        def _():
            xe[...] = zx
        @pl.when(gx == 0)
        def _():
            xw[...] = zx

    def rows(ref, y):
        return ref[pl.ds(y, LV, stride=H), :]

    temp_all[...] = jnp.zeros((LV * H, W), F32)
    temp_all[pl.ds(own, LO * H), :] = temp_ref[...]
    flow_all[:, pl.ds(own, LO * H), :] = flow_ref[...]
    clear_edges(cp1, xe1, xw1)
    clear_edges(cp2, xe2, xw2)

    def load(y, _):
        depth = ocean_ref[pl.ds(y, 1), :] * floor_ref[pl.ds(y, 1), :]
        cp1[WET, y + 2] = jnp.where(level < jnp.broadcast_to(depth, (LV, W)), 1.0, 0.0).astype(F32)
        for k in range(NT):
            cp1[1 + k, y + 2] = rows(c_ref.at[k], y)
        cp1[TF, y + 2] = rows(temp_all, y)
        return 0
    lax.fori_loop(0, H, load, 0)

    a1 = exchange(0, 0, cp1, xp1, xe1, xw1, 0, NT + 2)
    b1 = exchange(0, 1, cp1, xp1, xe1, xw1, UF, 2)
    a2 = exchange(1, 0, cp2, xp2, xe2, xw2, 1, NT + 1)
    b2 = exchange(1, 1, cp2, xp2, xe2, xw2, UF, 2)
    start(a1, (0, 1))
    pack(cp1, xp1, 0, NT + 2)
    start(a1, (2, 3))

    for cp in flows:
        cp.wait_recv()

    def load_flow(y, _):
        cp1[UF, y + 2] = rows(flow_all.at[0], y)
        cp1[VF, y + 2] = rows(flow_all.at[1], y)
        return 0
    lax.fori_loop(0, H, load_flow, 0)
    start(b1, (0, 1))
    pack(cp1, xp1, UF, 2)
    start(b1, (2, 3))
    wait_recv(a1)
    unpack(xp1, xe1, xw1, 0, NT + 2)
    wait_recv(b1)
    unpack(xp1, xe1, xw1, UF, 2)

    grid_rows = H * ny

    def halo(ref, f, y):
        return pltpu.roll(ref[f, y // SLOTS], W - 2 - 4 * lax.rem(y, SLOTS), 1)

    def sides(q, h):
        return (jnp.where(last, h, pltpu.roll(q, W - 1, 1)), jnp.where(first, h, pltpu.roll(q, 1, 1)))

    def currents(cp, store):
        def body(y, _):
            wet, wn, ws = cp1[WET, y + 2], cp1[WET, y + 3], cp1[WET, y + 1]
            u, un, us = cp[UF, y + 2], cp[UF, y + 3], cp[UF, y + 1]
            v, vn, vs = cp[VF, y + 2], cp[VF, y + 3], cp[VF, y + 1]
            we = coef[14, y]
            ww = coef[15, y]
            ue, uw = sides(u, halo(hc, UF, y))
            ve, vw = sides(v, halo(hc, VF, y))
            oe, on = wet * we, wet * wn
            cor = 0.1 + 0.1 * (gy * H + y).astype(F32) / grid_rows
            lap_u = ue + uw + un + us - 4.0 * u
            lap_v = ve + vw + vn + vs - 4.0 * v
            store(y, oe * (u + cor * v + viscosity * lap_u), on * (v - cor * u + viscosity * lap_v))
            U, V = oe * u, on * v
            Uw, Vs = wet * ww * uw, wet * ws * vs
            pe, me, pw, mw = jnp.maximum(U, 0.0), jnp.minimum(U, 0.0), jnp.maximum(Uw, 0.0), jnp.minimum(Uw, 0.0)
            pn, mn, ps, ms = jnp.maximum(V, 0.0), jnp.minimum(V, 0.0), jnp.maximum(Vs, 0.0), jnp.minimum(Vs, 0.0)
            coef[0, y] = wet * (1.0 - pe + mw - pn + ms)
            coef[1, y] = -(wet * me)
            coef[2, y] = wet * pw
            coef[3, y] = -0.5 * wet * (pe * (1.0 - U) + mw * (1.0 + Uw))
            coef[4, y] = 0.5 * wet * me * (1.0 + U)
            coef[5, y] = 0.5 * wet * pw * (1.0 - Uw)
            coef[6, y] = -(wet * mn)
            coef[7, y] = wet * ps
            coef[8, y] = -0.5 * wet * (pn * (1.0 - V) + ms * (1.0 + Vs))
            coef[9, y] = 0.5 * wet * mn * (1.0 + V)
            coef[10, y] = 0.5 * wet * ps * (1.0 - Vs)
            return 0
        lax.fori_loop(0, H, body, 0)

    def masks(y, _):
        wet = cp1[WET, y + 2]
        we, ww = sides(wet, halo(hc, WET, y))
        coef[14, y] = we
        coef[15, y] = ww
        below = jnp.where(level < LV - 1, pltpu.roll(wet, LV - 1, 0), 0.0)
        kv = rows(kv_ref, y) * wet * below
        up = pltpu.roll(kv, 1, 0)
        coef[11, y] = 1.0 - kv - up
        coef[12, y] = kv
        coef[13, y] = up
        return 0
    lax.fori_loop(0, H, masks, 0)

    def slopes_first(cp):
        for f in range(1, NT + 1):
            c = [cp[f, i] for i in range(4)]
            sy[f - 1, 0] = minmod(c[2] - c[1], c[1] - c[0])
            sy[f - 1, 1] = minmod(c[3] - c[2], c[2] - c[1])

    def advect(cp, f, y, co):
        c, cs, cn, cnn = cp[f, y + 2], cp[f, y + 1], cp[f, y + 3], cp[f, y + 4]
        sn = minmod(cnn - cn, cn - c)
        s0, ss = sy[f - 1, y + 1], sy[f - 1, y]
        sy[f - 1, y + 2] = sn
        ce, cw = sides(c, halo(hc, f, y))
        sx = minmod(ce - c, c - cw)
        se, sw = sides(sx, halo(hs, f, y))
        adv = ((co[0] * c + co[1] * ce) + (co[2] * cw + co[3] * sx)) + ((co[4] * se + co[5] * sw) + (
            co[6] * cn + co[7] * cs)) + ((co[8] * s0 + co[9] * sn) + co[10] * ss)
        return co[11] * adv + (co[12] * pltpu.roll(adv, LV - 1, 0) + co[13] * pltpu.roll(adv, 1, 0))

    def tracers(cp, dst, step):
        slopes_first(cp)
        sends = [[remote(part.at[step, pl.ds(q * CH, CH)], arecv.at[step, d - 1, pl.ds(q * CH, CH)],
                         asend.at[step, q, d], arec_sem.at[step, q, d],
                         {"tracer": lax.rem(t + d, nt)}) for d in range(1, nt)] for q in range(NCH)]

        def plankton(y, _):
            co = [coef[i, y] for i in range(14)]
            total = None
            for k in range(1, NT, 3):
                m = advect(cp, 1 + k, y, co)
                dst[1 + k, y + 2] = m
                total = m if total is None else total + m
            part[step, y] = total
            return 0

        def others(y, _):
            co = [coef[i, y] for i in range(14)]
            for k in range(NT):
                if k % 3 != 1:
                    dst[1 + k, y + 2] = advect(cp, 1 + k, y, co)
            return 0
        for q in range(NCH):
            lax.fori_loop(q * CH, (q + 1) * CH, plankton, 0)
            for cp_ in sends[q]:
                cp_.start()
        lax.fori_loop(0, H, others, 0)
        return sends

    def ecology(cp, mix, step, sends, put, put_temp):
        rate = [eco_ref[k] for k in range(NT)]

        def body(y, _):
            total = part[step, y]
            for d in range(nt - 1):
                total = total + arecv[step, d, y]
            a = water_absorb + plankton_absorb * total
            acc = a
            for sh in (1, 2, 4):
                if sh < LV:
                    acc = acc + jnp.where(level >= sh, pltpu.roll(acc, sh, 0), 0.0)
            tau = acc - a
            sol = jnp.broadcast_to(sol_ref[pl.ds(y, 1), :], (LV, W))
            light = sol * jnp.exp(-tau - 0.5 * a)
            heat = heat_share * sol * (jnp.exp(-tau) - jnp.exp(-tau - a))
            lim = light / (light + light_half)
            wet = cp1[WET, y + 2]
            for k in range(0, NT, 3):
                n, p, dt = mix[1 + k, y + 2], mix[2 + k, y + 2], mix[3 + k, y + 2]
                uptake = (rate[k] * lim) * p * n / (jnp.abs(n) + nutrient_half)
                dead, back = rate[k + 1] * p, rate[k + 2] * dt
                put(k, y, wet * (n - uptake + back))
                put(k + 1, y, wet * (p + uptake - dead))
                put(k + 2, y, wet * (dt + dead - back))
            tm = cp[TF, y + 2]
            te, tw = sides(tm, halo(hc, TF, y))
            put_temp(y, coef[0, y] * tm + coef[1, y] * te + coef[2, y] * tw
                     + coef[6, y] * cp[TF, y + 3] + coef[7, y] * cp[TF, y + 1] + wet * heat)
            return 0
        for q in range(NCH):
            for cp_ in sends[q]:
                cp_.wait_recv()
            lax.fori_loop(q * CH, (q + 1) * CH, body, 0)
        for q in range(NCH):
            for cp_ in sends[q]:
                cp_.wait_send()

    def store_next(y, u, v):
        cp2[UF, y + 2] = u
        cp2[VF, y + 2] = v
    currents(cp1, store_next)
    start(b2, (0, 1))
    pack(cp2, xp2, UF, 2)
    start(b2, (2, 3))
    sends = tracers(cp1, cp2, 0)

    def put_next(k, y, value):
        cp2[1 + k, y + 2] = value

    def put_temp_next(y, value):
        cp2[TF, y + 2] = value
    ecology(cp1, cp2, 0, sends, put_next, put_temp_next)
    start(a2, (0, 1))
    pack(cp2, xp2, 1, NT + 1)
    start(a2, (2, 3))

    wait_recv(b2)
    unpack(xp2, xe2, xw2, UF, 2)

    def store_last(y, u, v):
        flow_out[0, pl.ds(y, LV, stride=H), :] = u
        flow_out[1, pl.ds(y, LV, stride=H), :] = v
    currents(cp2, store_last)
    outf_ref[...] = flow_out[:, pl.ds(own, LO * H), :]
    wait_send(a1)
    wait_send(b1)
    for cp in flows:
        cp.wait_send()
    wait_recv(a2)
    unpack(xp2, xe2, xw2, 1, NT + 1)
    sends = tracers(cp2, cp1, 1)

    def put_last(k, y, value):
        out_ref[k, pl.ds(y, LV, stride=H), :] = value

    def put_temp_last(y, value):
        temp_all[pl.ds(y, LV, stride=H), :] = value
    ecology(cp2, cp1, 1, sends, put_last, put_temp_last)
    outt_ref[...] = temp_all[pl.ds(own, LO * H), :]
    wait_send(a2)
    wait_send(b2)


def per_device(nx, ny, nt, c, flow, temp, kv, sol, eco, ocean, floor):
    NT, LV, H, W = c.shape
    LO = temp.shape[0]
    NF, G = NT + 4, H // SLOTS
    assert H % SLOTS == 0 and W == 4 * SLOTS
    NCH = 4
    vm = pltpu.VMEM
    dma = pltpu.SemaphoreType.DMA
    field = vm((NF, H + 4, LV, W), F32)
    edge = vm((NF, G, LV, W), F32)
    whole = pl.BlockSpec(memory_space=pltpu.VMEM)
    out, outf, outt = pl.pallas_call(
        functools.partial(kernel, nx, ny, nt, NT, LV, LO, H, W),
        out_shape=(jax.ShapeDtypeStruct((NT, LV * H, W), F32),
                   jax.ShapeDtypeStruct((2, LO * H, W), F32),
                   jax.ShapeDtypeStruct((LO * H, W), F32)),
        in_specs=[whole] * 5 + [pl.BlockSpec(memory_space=pltpu.SMEM)] + [whole] * 2,
        out_specs=(whole,) * 3,
        scratch_shapes=[field, field, edge, edge, edge, edge, edge, edge, edge, edge,
                        vm((2, LV * H, W), F32), vm((LV * H, W), F32), vm((2, LV * H, W), F32),
                        vm((16, H, LV, W), F32), vm((NT, H + 2, LV, W), F32),
                        vm((STEPS, H, LV, W), F32), vm((STEPS, max(nt - 1, 1), H, LV, W), F32),
                        dma((nt,)), dma((nt,)), dma((STEPS, 2, 4)), dma((STEPS, 2, 4)),
                        dma((STEPS, NCH, nt)), dma((STEPS, NCH, nt))],
        compiler_params=pltpu.CompilerParams(collective_id=0, has_side_effects=True,
                                             vmem_limit_bytes=60 * 1024 * 1024),
        name="ocean",
    )(c.reshape(NT, LV * H, W), flow.reshape(2, LO * H, W), temp.reshape(LO * H, W),
      kv.reshape(LV * H, W), sol, eco, ocean, floor)
    return out.reshape(c.shape), outf.reshape(flow.shape), outt.reshape(temp.shape)


def solution(mesh):
    in_specs = (
        P("tracer", None, "gy", "gx"),
        P(None, "tracer", "gy", "gx"),
        P("tracer", "gy", "gx"),
        P(None, "gy", "gx"),
        P("gy", "gx"),
        P("tracer"),
        P("gy", "gx"),
        P("gy", "gx"),
    )
    out_specs = (
        P("tracer", None, "gy", "gx"),
        P(None, "tracer", "gy", "gx"),
        P("tracer", "gy", "gx"),
    )
    body = functools.partial(per_device, mesh.shape["gx"], mesh.shape["gy"], mesh.shape["tracer"])
    return jax.shard_map(body, mesh=mesh, in_specs=in_specs, out_specs=out_specs, check_vma=False)
```

profile of v0, /device:TPU:0, one launch (start us, length us, event | category | flops | bytes accessed | tf_op | source)
XLA Modules:
  0.0 100.5 jit_solution(1073640786777507208)
XLA Ops:
  0.6 94.5 %ocean.1 = (f32[12,512,128]{2,1,0:T(8,128)}, f32[2,256,128]{2,1,0:T(8,128)}, f32[256,128]{1,0:T(8,128)}) custom-call(f32[12,512,128]{2,1,0:T(8,128)} %bitcast.8, f32[2,256,128]{2,1,0:T(8,128)} %bitcast.9, f32[256,128]{1,0:T(8,128)} %bitcast.12, f32[512,128]{1,0:T(8,128)} %bitcast.10, f32[64,128]{1,0:T(8,128)} %sol_ref.1, f32[12]{0:T(128)} %eco_ref.1, ...), custom_call_target="tpu_custom_call" | custom-call | tf_op jit(solution)/shard_map/ocean/pallas_call | solution.py:370
  95.1 0.0 copy-start
  95.1 0.0 copy-start.1
  95.2 4.0 %copy.14 = f32[12,8,64,128]{3,2,1,0:T(8,128)} copy(f32[12,8,64,128]{3,2,1,0:T(8,128)} %bitcast.7) | data formatting | bytes 6291456
  99.2 0.0 copy-done
  99.2 0.7 copy.15
  99.9 0.0 copy-done.1
  99.9 0.7 copy.16
Async XLA Ops:
  95.1 4.0 %copy-start = (f32[2,256,128]{2,1,0:T(8,128)S(1)}, f32[2,256,128]{2,1,0:T(8,128)}, u32[]{:S(2)}) copy-start(f32[2,256,128]{2,1,0:T(8,128)} %get-tuple-element.7) | copy-start | bytes 786436
  95.1 4.7 %copy-start.1 = (f32[256,128]{1,0:T(8,128)S(1)}, f32[256,128]{1,0:T(8,128)}, u32[]{:S(2)}) copy-start(f32[256,128]{1,0:T(8,128)} %get-tuple-element.8) | copy-start | bytes 393220
where the time goes:
time: 101 us
  Pallas kernels  94.5 us (94%)
  local copies, waits for them, and re-layouts  5.38 us (5%)
    pallas_call x1, Pallas kernels, per_device(): pl.pallas_call(functools.partial(kernel, nx, ny, nt, NT, LV, LO, H, W), o...  94.5 us
    unnamed x7, local copies, waits for them, and re-layouts  5.38 us

commit v1 on v0

--- a/solution.py
+++ b/solution.py
@@ -15,6 +15,7 @@
 light_half = 0.3
 nutrient_half = 0.5
 SLOTS = 32
+ROWS = 8
 F32 = jnp.float32
 
 
@@ -26,7 +27,7 @@
            c_ref, flow_ref, temp_ref, kv_ref, sol_ref, eco_ref, ocean_ref, floor_ref,
            out_ref, outf_ref, outt_ref,
            cp1, cp2, xp1, xp2, xe1, xe2, xw1, xw2, hc, hs,
-           flow_all, temp_all, flow_out, coef, sy, part, arecv,
+           flow_all, temp_all, flow_out, coef, part, arecv,
            fs, fr, hsend, hrecv, asend, arec_sem):
     gx, gy, t = lax.axis_index("gx"), lax.axis_index("gy"), lax.axis_index("tracer")
     WET, TF, UF, VF = 0, NT + 1, NT + 2, NT + 3
@@ -129,6 +130,13 @@
         def _():
             xw[...] = zx
 
+    def each_row(lo, hi, n, fn):
+        def body(i, _):
+            for r in range(n):
+                fn(i * n + r, 0)
+            return 0
+        lax.fori_loop(lo // n, hi // n, body, 0)
+
     def rows(ref, y):
         return ref[pl.ds(y, LV, stride=H), :]
 
@@ -145,7 +153,7 @@
             cp1[1 + k, y + 2] = rows(c_ref.at[k], y)
         cp1[TF, y + 2] = rows(temp_all, y)
         return 0
-    lax.fori_loop(0, H, load, 0)
+    each_row(0, H, 2, load)
 
     a1 = exchange(0, 0, cp1, xp1, xe1, xw1, 0, NT + 2)
     b1 = exchange(0, 1, cp1, xp1, xe1, xw1, UF, 2)
@@ -162,7 +170,7 @@
         cp1[UF, y + 2] = rows(flow_all.at[0], y)
         cp1[VF, y + 2] = rows(flow_all.at[1], y)
         return 0
-    lax.fori_loop(0, H, load_flow, 0)
+    each_row(0, H, 8, load_flow)
     start(b1, (0, 1))
     pack(cp1, xp1, UF, 2)
     start(b1, (2, 3))
@@ -209,7 +217,7 @@
             coef[9, y] = 0.5 * wet * mn * (1.0 + V)
             coef[10, y] = 0.5 * wet * ps * (1.0 - Vs)
             return 0
-        lax.fori_loop(0, H, body, 0)
+        each_row(0, H, 4, body)
 
     def masks(y, _):
         wet = cp1[WET, y + 2]
@@ -223,53 +231,60 @@
         coef[12, y] = kv
         coef[13, y] = up
         return 0
-    lax.fori_loop(0, H, masks, 0)
-
-    def slopes_first(cp):
-        for f in range(1, NT + 1):
-            c = [cp[f, i] for i in range(4)]
-            sy[f - 1, 0] = minmod(c[2] - c[1], c[1] - c[0])
-            sy[f - 1, 1] = minmod(c[3] - c[2], c[2] - c[1])
-
-    def advect(cp, f, y, co):
-        c, cs, cn, cnn = cp[f, y + 2], cp[f, y + 1], cp[f, y + 3], cp[f, y + 4]
-        sn = minmod(cnn - cn, cn - c)
-        s0, ss = sy[f - 1, y + 1], sy[f - 1, y]
-        sy[f - 1, y + 2] = sn
-        ce, cw = sides(c, halo(hc, f, y))
-        sx = minmod(ce - c, c - cw)
-        se, sw = sides(sx, halo(hs, f, y))
-        adv = ((co[0] * c + co[1] * ce) + (co[2] * cw + co[3] * sx)) + ((co[4] * se + co[5] * sw) + (
-            co[6] * cn + co[7] * cs)) + ((co[8] * s0 + co[9] * sn) + co[10] * ss)
-        return co[11] * adv + (co[12] * pltpu.roll(adv, LV - 1, 0) + co[13] * pltpu.roll(adv, 1, 0))
+    each_row(0, H, 8, masks)
+
+    def advect(cp, f, b):
+        base = b * ROWS
+        c = [cp[f, base + i] for i in range(ROWS + 4)]
+        d = [c[i + 1] - c[i] for i in range(ROWS + 3)]
+        s = [minmod(d[i + 1], d[i]) for i in range(ROWS + 2)]
+        group = base // SLOTS
+        near, slope = hc[f, group], hs[f, group]
+        turn = W - 2 - 4 * lax.rem(base, SLOTS)
+        out = []
+        for r in range(ROWS):
+            y = base + r
+            m = c[r + 2]
+            ce, cw = sides(m, pltpu.roll(near, turn - 4 * r, 1))
+            sx = minmod(ce - m, m - cw)
+            se, sw = sides(sx, pltpu.roll(slope, turn - 4 * r, 1))
+            x = (coef[0, y] * m + coef[1, y] * ce) + (coef[2, y] * cw + coef[3, y] * sx)
+            x = x + (coef[4, y] * se + coef[5, y] * sw)
+            z = (coef[6, y] * c[r + 3] + coef[7, y] * c[r + 1]) + (coef[8, y] * s[r + 1] + coef[9, y] * s[r + 2])
+            adv = x + (z + coef[10, y] * s[r])
+            out.append(coef[11, y] * adv + (coef[12, y] * pltpu.roll(adv, LV - 1, 0)
+                                            + coef[13, y] * pltpu.roll(adv, 1, 0)))
+        return out
 
     def tracers(cp, dst, step):
-        slopes_first(cp)
         sends = [[remote(part.at[step, pl.ds(q * CH, CH)], arecv.at[step, d - 1, pl.ds(q * CH, CH)],
                          asend.at[step, q, d], arec_sem.at[step, q, d],
                          {"tracer": lax.rem(t + d, nt)}) for d in range(1, nt)] for q in range(NCH)]
 
-        def plankton(y, _):
-            co = [coef[i, y] for i in range(14)]
+        def plankton(b, _):
             total = None
             for k in range(1, NT, 3):
-                m = advect(cp, 1 + k, y, co)
-                dst[1 + k, y + 2] = m
-                total = m if total is None else total + m
-            part[step, y] = total
-            return 0
-
-        def others(y, _):
-            co = [coef[i, y] for i in range(14)]
+                m = advect(cp, 1 + k, b)
+                for r in range(ROWS):
+                    dst[1 + k, b * ROWS + r + 2] = m[r]
+                total = m if total is None else [p + q for p, q in zip(total, m)]
+            for r in range(ROWS):
+                part[step, b * ROWS + r] = total[r]
+            return 0
+
+        def others(b, _):
             for k in range(NT):
                 if k % 3 != 1:
-                    dst[1 + k, y + 2] = advect(cp, 1 + k, y, co)
-            return 0
+                    m = advect(cp, 1 + k, b)
+                    for r in range(ROWS):
+                        dst[1 + k, b * ROWS + r + 2] = m[r]
+            return 0
+        BC = CH // ROWS
         for q in range(NCH):
-            lax.fori_loop(q * CH, (q + 1) * CH, plankton, 0)
+            lax.fori_loop(q * BC, (q + 1) * BC, plankton, 0)
             for cp_ in sends[q]:
                 cp_.start()
-        lax.fori_loop(0, H, others, 0)
+        lax.fori_loop(0, H // ROWS, others, 0)
         return sends
 
     def ecology(cp, mix, step, sends, put, put_temp):
@@ -305,7 +320,7 @@
         for q in range(NCH):
             for cp_ in sends[q]:
                 cp_.wait_recv()
-            lax.fori_loop(q * CH, (q + 1) * CH, body, 0)
+            each_row(q * CH, (q + 1) * CH, 4, body)
         for q in range(NCH):
             for cp_ in sends[q]:
                 cp_.wait_send()
@@ -376,7 +391,7 @@
         out_specs=(whole,) * 3,
         scratch_shapes=[field, field, edge, edge, edge, edge, edge, edge, edge, edge,
                         vm((2, LV * H, W), F32), vm((LV * H, W), F32), vm((2, LV * H, W), F32),
-                        vm((16, H, LV, W), F32), vm((NT, H + 2, LV, W), F32),
+                        vm((16, H, LV, W), F32),
                         vm((STEPS, H, LV, W), F32), vm((STEPS, max(nt - 1, 1), H, LV, W), F32),
                         dma((nt,)), dma((nt,)), dma((STEPS, 2, 4)), dma((STEPS, 2, 4)),
                         dma((STEPS, NCH, nt)), dma((STEPS, NCH, nt))],

time: 101 us -> 105 us (1.040)
  Pallas kernels: 94.5 us -> 98.5 us
    pallas_call x1, Pallas kernels: 94.5 us -> 98.5 us  [per_device(): pl.pallas_call(functools.partial(kernel, nx, ny, nt, NT, LV, LO, H, W), o...]
where the time goes in v1:
time: 105 us
  Pallas kernels  98.5 us (94%)
  local copies, waits for them, and re-layouts  5.38 us (5%)
    pallas_call x1, Pallas kernels, per_device(): pl.pallas_call(functools.partial(kernel, nx, ny, nt, NT, LV, LO, H, W), o...  98.5 us
    unnamed x7, local copies, waits for them, and re-layouts  5.38 us

profile of v1, /device:TPU:0, one launch (start us, length us, event | category | flops | bytes accessed | tf_op | source)
XLA Modules:
  0.0 104.5 jit_solution(9321543586010581380)
XLA Ops:
  0.6 98.5 %ocean.1 = (f32[12,512,128]{2,1,0:T(8,128)}, f32[2,256,128]{2,1,0:T(8,128)}, f32[256,128]{1,0:T(8,128)}) custom-call(f32[12,512,128]{2,1,0:T(8,128)} %bitcast.8, f32[2,256,128]{2,1,0:T(8,128)} %bitcast.9, f32[256,128]{1,0:T(8,128)} %bitcast.12, f32[512,128]{1,0:T(8,128)} %bitcast.10, f32[64,128]{1,0:T(8,128)} %sol_ref.1, f32[12]{0:T(128)} %eco_ref.1, ...), custom_call_target="tpu_custom_call" | custom-call | tf_op jit(solution)/shard_map/ocean/pallas_call | solution.py:385
  99.1 0.0 copy-start
  99.2 0.0 copy-start.1
  99.2 4.0 %copy.14 = f32[12,8,64,128]{3,2,1,0:T(8,128)} copy(f32[12,8,64,128]{3,2,1,0:T(8,128)} %bitcast.7) | data formatting | bytes 6291456
  103.2 0.0 copy-done
  103.2 0.7 copy.15
  103.9 0.0 copy-done.1
  103.9 0.7 copy.16
Async XLA Ops:
  99.1 4.0 %copy-start = (f32[2,256,128]{2,1,0:T(8,128)S(1)}, f32[2,256,128]{2,1,0:T(8,128)}, u32[]{:S(2)}) copy-start(f32[2,256,128]{2,1,0:T(8,128)} %get-tuple-element.7) | copy-start | bytes 786436
  99.2 4.7 %copy-start.1 = (f32[256,128]{1,0:T(8,128)S(1)}, f32[256,128]{1,0:T(8,128)}, u32[]{:S(2)}) copy-start(f32[256,128]{1,0:T(8,128)} %get-tuple-element.8) | copy-start | bytes 393220

commit v2 on v1

--- a/solution.py
+++ b/solution.py
@@ -15,7 +15,6 @@
 light_half = 0.3
 nutrient_half = 0.5
 SLOTS = 32
-ROWS = 8
 F32 = jnp.float32
 
 
@@ -24,7 +23,7 @@
 
 
 def kernel(nx, ny, nt, NT, LV, LO, H, W,
-           c_ref, flow_ref, temp_ref, kv_ref, sol_ref, eco_ref, ocean_ref, floor_ref,
+           c_ref, flow_ref, temp_ref, kv_ref, sol_ref, eco_ref, ocean_ref, floor_ref, shift_ref,
            out_ref, outf_ref, outt_ref,
            cp1, cp2, xp1, xp2, xe1, xe2, xw1, xw2, hc, hs,
            flow_all, temp_all, flow_out, coef, part, arecv,
@@ -233,58 +232,59 @@
         return 0
     each_row(0, H, 8, masks)
 
-    def advect(cp, f, b):
-        base = b * ROWS
-        c = [cp[f, base + i] for i in range(ROWS + 4)]
-        d = [c[i + 1] - c[i] for i in range(ROWS + 3)]
-        s = [minmod(d[i + 1], d[i]) for i in range(ROWS + 2)]
-        group = base // SLOTS
-        near, slope = hc[f, group], hs[f, group]
-        turn = W - 2 - 4 * lax.rem(base, SLOTS)
-        out = []
-        for r in range(ROWS):
-            y = base + r
-            m = c[r + 2]
-            ce, cw = sides(m, pltpu.roll(near, turn - 4 * r, 1))
-            sx = minmod(ce - m, m - cw)
-            se, sw = sides(sx, pltpu.roll(slope, turn - 4 * r, 1))
-            x = (coef[0, y] * m + coef[1, y] * ce) + (coef[2, y] * cw + coef[3, y] * sx)
-            x = x + (coef[4, y] * se + coef[5, y] * sw)
-            z = (coef[6, y] * c[r + 3] + coef[7, y] * c[r + 1]) + (coef[8, y] * s[r + 1] + coef[9, y] * s[r + 2])
-            adv = x + (z + coef[10, y] * s[r])
-            out.append(coef[11, y] * adv + (coef[12, y] * pltpu.roll(adv, LV - 1, 0)
-                                            + coef[13, y] * pltpu.roll(adv, 1, 0)))
-        return out
+    cells = (SLOTS, LV, W)
+    flat = (SLOTS * LV, W)
+    own_slot = lax.broadcasted_iota(jnp.int32, cells, 0) == lax.broadcasted_iota(jnp.int32, cells, 2) // 4
+
+    def spread(edge):
+        return jnp.where(own_slot, jnp.broadcast_to(edge[None], cells), 0.0).reshape(flat)
+
+    def moved(x):
+        return jnp.dot(x, shift_ref[...], preferred_element_type=F32)
+
+    def advect(cp, dst, f, g, total):
+        base = g * SLOTS
+        c = cp[f, pl.ds(base + 2, SLOTS)].reshape(flat)
+        x = jnp.concatenate([c, spread(hc[f, g])], 1)
+        high = x.astype(jnp.bfloat16)
+        low = (x - high.astype(F32)).astype(jnp.bfloat16)
+        pair = moved(high) + moved(low)
+        ce, cw = pair[:, :W], pair[:, W:]
+        sx = minmod(ce - c, c - cw)
+        spair = moved(jnp.concatenate([sx, spread(hs[f, g])], 1).astype(jnp.bfloat16))
+        d = cp[f, pl.ds(base + 1, SLOTS + 3)] - cp[f, pl.ds(base, SLOTS + 3)]
+        s = minmod(d[1:], d[:-1])
+        for r in range(SLOTS):
+            y, w = base + r, slice(r * LV, (r + 1) * LV)
+            z = (coef[0, y] * c[w] + coef[1, y] * ce[w]) + (coef[2, y] * cw[w] + coef[3, y] * sx[w])
+            z = z + (coef[4, y] * spair[w, :W] + coef[5, y] * spair[w, W:])
+            z = z + (coef[6, y] * cp[f, y + 3] + coef[7, y] * cp[f, y + 1])
+            adv = z + ((coef[8, y] * s[r + 1] + coef[9, y] * s[r + 2]) + coef[10, y] * s[r])
+            m = coef[11, y] * adv + (coef[12, y] * pltpu.roll(adv, LV - 1, 0)
+                                     + coef[13, y] * pltpu.roll(adv, 1, 0))
+            dst[f, y + 2] = m
+            if total is not None:
+                part[total, y] = part[total, y] + m
 
     def tracers(cp, dst, step):
         sends = [[remote(part.at[step, pl.ds(q * CH, CH)], arecv.at[step, d - 1, pl.ds(q * CH, CH)],
                          asend.at[step, q, d], arec_sem.at[step, q, d],
                          {"tracer": lax.rem(t + d, nt)}) for d in range(1, nt)] for q in range(NCH)]
-
-        def plankton(b, _):
-            total = None
-            for k in range(1, NT, 3):
-                m = advect(cp, 1 + k, b)
-                for r in range(ROWS):
-                    dst[1 + k, b * ROWS + r + 2] = m[r]
-                total = m if total is None else [p + q for p, q in zip(total, m)]
-            for r in range(ROWS):
-                part[step, b * ROWS + r] = total[r]
-            return 0
-
-        def others(b, _):
-            for k in range(NT):
-                if k % 3 != 1:
-                    m = advect(cp, 1 + k, b)
-                    for r in range(ROWS):
-                        dst[1 + k, b * ROWS + r + 2] = m[r]
-            return 0
-        BC = CH // ROWS
+        part[step] = jnp.zeros((H, LV, W), F32)
+
+        def plankton(i, _):
+            advect(cp, dst, 2 + 3 * (i // G), lax.rem(i, G), step)
+            return 0
+
+        def others(i, _):
+            q = i // G
+            advect(cp, dst, 1 + 3 * (q // 2) + 2 * lax.rem(q, 2), lax.rem(i, G), None)
+            return 0
+        lax.fori_loop(0, NT // 3 * G, plankton, 0)
         for q in range(NCH):
-            lax.fori_loop(q * BC, (q + 1) * BC, plankton, 0)
             for cp_ in sends[q]:
                 cp_.start()
-        lax.fori_loop(0, H // ROWS, others, 0)
+        lax.fori_loop(0, NT // 3 * 2 * G, others, 0)
         return sends
 
     def ecology(cp, mix, step, sends, put, put_temp):
@@ -371,6 +371,14 @@
     wait_send(b2)
 
 
+def shift_matrix(W):
+    k, n = lax.broadcasted_iota(jnp.int32, (2 * W, 2 * W), 0), lax.broadcasted_iota(jnp.int32, (2 * W, 2 * W), 1)
+    inside, edge = k < W, (k >= W)
+    east = jnp.where(n < W - 1, inside & (k == n + 1), (n == W - 1) & edge & (k % 4 == 1))
+    west = jnp.where(n > W, inside & (k == n - W - 1), (n == W) & edge & (k % 4 == 2))
+    return jnp.where(n < W, east, west).astype(jnp.bfloat16)
+
+
 def per_device(nx, ny, nt, c, flow, temp, kv, sol, eco, ocean, floor):
     NT, LV, H, W = c.shape
     LO = temp.shape[0]
@@ -387,7 +395,7 @@
         out_shape=(jax.ShapeDtypeStruct((NT, LV * H, W), F32),
                    jax.ShapeDtypeStruct((2, LO * H, W), F32),
                    jax.ShapeDtypeStruct((LO * H, W), F32)),
-        in_specs=[whole] * 5 + [pl.BlockSpec(memory_space=pltpu.SMEM)] + [whole] * 2,
+        in_specs=[whole] * 5 + [pl.BlockSpec(memory_space=pltpu.SMEM)] + [whole] * 3,
         out_specs=(whole,) * 3,
         scratch_shapes=[field, field, edge, edge, edge, edge, edge, edge, edge, edge,
                         vm((2, LV * H, W), F32), vm((LV * H, W), F32), vm((2, LV * H, W), F32),
@@ -399,7 +407,7 @@
                                              vmem_limit_bytes=60 * 1024 * 1024),
         name="ocean",
     )(c.reshape(NT, LV * H, W), flow.reshape(2, LO * H, W), temp.reshape(LO * H, W),
-      kv.reshape(LV * H, W), sol, eco, ocean, floor)
+      kv.reshape(LV * H, W), sol, eco, ocean, floor, shift_matrix(W))
     return out.reshape(c.shape), outf.reshape(flow.shape), outt.reshape(temp.shape)
 
 

time: 105 us -> 62 us (0.59)
  Pallas kernels: 98.5 us -> 54.8 us
    pallas_call x1, Pallas kernels: 98.5 us -> 54.8 us  [per_device(): pl.pallas_call(functools.partial(kernel, nx, ny, nt, NT, LV, LO, H, W), o...]
where the time goes in v2:
time: 62 us; the launch traced here: 61.9 us
  Pallas kernels  54.8 us (88%)
  local copies, waits for them, and re-layouts  5.38 us (9%)
  other arithmetic  0.94 us (2%)
  between operations  0.69 us (1%)
    pallas_call x1, Pallas kernels, per_device(): pl.pallas_call(functools.partial(kernel, nx, ny, nt, NT, LV, LO, H, W), o...  54.8 us
    unnamed x7, local copies, waits for them, and re-layouts  5.38 us

profile of v2, /device:TPU:0, one launch (start us, length us, event | category | flops | bytes accessed | tf_op | source)
XLA Modules:
  0.0 61.9 jit_solution(16478922384273622354)
XLA Ops:
  0.7 0.9 %fusion.3.shift_ref = bf16[256,256]{1,0:T(8,128)(2,1)} fusion(s32[256]{0:T(256)S(1)} %get-tuple-element.11, s32[256]{0:T(256)S(1)} %get-tuple-element.17, s32[256]{0:T(256)S(1)} %get-tuple-element.18, s32[256]{0:T(256)S(1)} %get-tuple-element.12, pred[256]{0:T(512)(128)(4,1)S(1)} %get-tuple-element.16, pred[256]{0:T(512)(128)(4,1)S(1)} %get-tuple-element.15, ...), kind=kLoop, calls=%fused_computation.7 | loop fusion | flops 983040 | bytes 136960 | tf_op jit(solution)/shard_map/convert_element_type | solution.py:379
  1.6 54.8 %ocean.1 = (f32[12,512,128]{2,1,0:T(8,128)}, f32[2,256,128]{2,1,0:T(8,128)}, f32[256,128]{1,0:T(8,128)}) custom-call(f32[12,512,128]{2,1,0:T(8,128)} %bitcast.8, f32[2,256,128]{2,1,0:T(8,128)} %bitcast.9, f32[256,128]{1,0:T(8,128)} %bitcast.12, f32[512,128]{1,0:T(8,128)} %bitcast.10, f32[64,128]{1,0:T(8,128)} %sol_ref.1, f32[12]{0:T(128)} %eco_ref.1, ...), custom_call_target="tpu_custom_call" | custom-call | tf_op jit(solution)/shard_map/ocean/pallas_call | solution.py:393
  56.5 0.0 copy-start
  56.5 0.0 copy-start.1
  56.5 4.0 %copy.14 = f32[12,8,64,128]{3,2,1,0:T(8,128)} copy(f32[12,8,64,128]{3,2,1,0:T(8,128)} %bitcast.7) | data formatting | bytes 6291456
  60.5 0.0 copy-done
  60.5 0.7 %copy.15 = f32[2,4,64,128]{3,2,1,0:T(8,128)} copy(f32[2,4,64,128]{3,2,1,0:T(8,128)S(1)} %bitcast.11) | data formatting | bytes 524288
  61.2 0.0 copy-done.1
  61.2 0.7 %copy.16 = f32[4,64,128]{2,1,0:T(8,128)} copy(f32[4,64,128]{2,1,0:T(8,128)S(1)} %bitcast.13) | data formatting | bytes 262144
  (6 shorter events, 0.0 us)
Async XLA Ops:
  56.5 4.0 %copy-start = (f32[2,256,128]{2,1,0:T(8,128)S(1)}, f32[2,256,128]{2,1,0:T(8,128)}, u32[]{:S(2)}) copy-start(f32[2,256,128]{2,1,0:T(8,128)} %get-tuple-element.7) | copy-start | bytes 786436
  56.5 4.7 %copy-start.1 = (f32[256,128]{1,0:T(8,128)S(1)}, f32[256,128]{1,0:T(8,128)}, u32[]{:S(2)}) copy-start(f32[256,128]{1,0:T(8,128)} %get-tuple-element.8) | copy-start | bytes 393220

commit v3 on v2

--- a/solution.py
+++ b/solution.py
@@ -23,7 +23,7 @@
 
 
 def kernel(nx, ny, nt, NT, LV, LO, H, W,
-           c_ref, flow_ref, temp_ref, kv_ref, sol_ref, eco_ref, ocean_ref, floor_ref, shift_ref,
+           c_ref, flow_ref, temp_ref, kv_ref, sol_ref, eco_ref, ocean_ref, floor_ref, shift_ref, ends_ref,
            out_ref, outf_ref, outt_ref,
            cp1, cp2, xp1, xp2, xe1, xe2, xw1, xw2, hc, hs,
            flow_all, temp_all, flow_out, coef, part, arecv,
@@ -93,10 +93,13 @@
     def pack(cp, xp, lo, n):
         def body(f, _):
             for g in range(G):
-                acc = jnp.zeros((LV, W), F32)
-                for j in range(SLOTS):
-                    row = cp[f, 2 + g * SLOTS + j]
-                    acc = jnp.where(lane_slot == j, pltpu.roll(row, (4 * j + 2) % W, 1), acc)
+                c = cp[f, pl.ds(2 + g * SLOTS, SLOTS)].reshape(SLOTS * LV, W)
+                high = c.astype(jnp.bfloat16)
+                low = (c - high.astype(F32)).astype(jnp.bfloat16)
+                ends = jnp.dot(jnp.concatenate([high, low], 1), ends_ref[...], preferred_element_type=F32)
+                acc = ends[:LV]
+                for j in range(1, SLOTS):
+                    acc = jnp.where(lane_slot == j, ends[j * LV:(j + 1) * LV], acc)
                 xp[f, g] = acc
             return 0
         lax.fori_loop(lo, lo + n, body, 0)
@@ -379,6 +382,11 @@
     return jnp.where(n < W, east, west).astype(jnp.bfloat16)
 
 
+def ends_matrix(W):
+    k, n = lax.broadcasted_iota(jnp.int32, (2 * W, W), 0), lax.broadcasted_iota(jnp.int32, (2 * W, W), 1)
+    return (k % W == (n % 4 + W - 2) % W).astype(jnp.bfloat16)
+
+
 def per_device(nx, ny, nt, c, flow, temp, kv, sol, eco, ocean, floor):
     NT, LV, H, W = c.shape
     LO = temp.shape[0]
@@ -395,7 +403,7 @@
         out_shape=(jax.ShapeDtypeStruct((NT, LV * H, W), F32),
                    jax.ShapeDtypeStruct((2, LO * H, W), F32),
                    jax.ShapeDtypeStruct((LO * H, W), F32)),
-        in_specs=[whole] * 5 + [pl.BlockSpec(memory_space=pltpu.SMEM)] + [whole] * 3,
+        in_specs=[whole] * 5 + [pl.BlockSpec(memory_space=pltpu.SMEM)] + [whole] * 4,
         out_specs=(whole,) * 3,
         scratch_shapes=[field, field, edge, edge, edge, edge, edge, edge, edge, edge,
                         vm((2, LV * H, W), F32), vm((LV * H, W), F32), vm((2, LV * H, W), F32),
@@ -407,7 +415,7 @@
                                              vmem_limit_bytes=60 * 1024 * 1024),
         name="ocean",
     )(c.reshape(NT, LV * H, W), flow.reshape(2, LO * H, W), temp.reshape(LO * H, W),
-      kv.reshape(LV * H, W), sol, eco, ocean, floor, shift_matrix(W))
+      kv.reshape(LV * H, W), sol, eco, ocean, floor, shift_matrix(W), ends_matrix(W))
     return out.reshape(c.shape), outf.reshape(flow.shape), outt.reshape(temp.shape)
 
 

time: 62 us -> 64.8 us (1.045)
  Pallas kernels: 54.8 us -> 56.8 us
  other arithmetic: 0.94 us -> 1.75 us
    pallas_call x1, Pallas kernels: 54.8 us -> 56.8 us  [per_device(): pl.pallas_call(functools.partial(kernel, nx, ny, nt, NT, LV, LO, H, W), o...]
    convert_element_type x0 -> x1, other arithmetic: none -> 0.8 us  [ends_matrix(): return (k % W == (n % 4 + W - 2) % W).astype(jnp.bfloat16)]
where the time goes in v3:
time: 64.8 us; the launch traced here: 64.7 us
  Pallas kernels  56.8 us (88%)
  local copies, waits for them, and re-layouts  5.38 us (8%)
  other arithmetic  1.75 us (3%)
  between operations  0.72 us (1%)
    pallas_call x1, Pallas kernels, per_device(): pl.pallas_call(functools.partial(kernel, nx, ny, nt, NT, LV, LO, H, W), o...  56.8 us
    unnamed x7, local copies, waits for them, and re-layouts  5.38 us

profile of v3, /device:TPU:0, one launch (start us, length us, event | category | flops | bytes accessed | tf_op | source)
XLA Modules:
  0.0 64.7 jit_solution(5982698802884687516)
XLA Ops:
  0.7 0.8 %fusion.10.ends_ref = bf16[256,128]{1,0:T(8,128)(2,1)} fusion(s32[128]{0:T(128)S(1)} %get-tuple-element.21, s32[128]{0:T(128)S(1)} %get-tuple-element.22, s32[256]{0:T(256)S(1)} %get-tuple-element.19, s32[256]{0:T(256)S(1)} %get-tuple-element.20, pred[256]{0:T(512)(128)(4,1)S(1)} %compare_and_fusion.1, pred[128]{0:T(512)(128)(4,1)S(1)} %compare_and_fusion), kind=kLoop, calls=%fused_computation.17 | loop fusion | flops 524288 | bytes 68992 | tf_op jit(solution)/shard_map/convert_element_type | solution.py:387
  1.5 0.9 %fusion.3.shift_ref = bf16[256,256]{1,0:T(8,128)(2,1)} fusion(s32[256]{0:T(256)S(1)} %get-tuple-element.11, s32[256]{0:T(256)S(1)} %get-tuple-element.17, s32[256]{0:T(256)S(1)} %get-tuple-element.18, s32[256]{0:T(256)S(1)} %get-tuple-element.12, pred[256]{0:T(512)(128)(4,1)S(1)} %get-tuple-element.16, pred[256]{0:T(512)(128)(4,1)S(1)} %get-tuple-element.15, ...), kind=kLoop, calls=%fused_computation.7 | loop fusion | flops 983040 | bytes 136960 | tf_op jit(solution)/shard_map/convert_element_type | solution.py:382
  2.4 56.8 %ocean.1 = (f32[12,512,128]{2,1,0:T(8,128)}, f32[2,256,128]{2,1,0:T(8,128)}, f32[256,128]{1,0:T(8,128)}) custom-call(f32[12,512,128]{2,1,0:T(8,128)} %bitcast.8, f32[2,256,128]{2,1,0:T(8,128)} %bitcast.9, f32[256,128]{1,0:T(8,128)} %bitcast.12, f32[512,128]{1,0:T(8,128)} %bitcast.10, f32[64,128]{1,0:T(8,128)} %sol_ref.1, f32[12]{0:T(128)} %eco_ref.1, ...), custom_call_target="tpu_custom_call" | custom-call | tf_op jit(solution)/shard_map/ocean/pallas_call | solution.py:401
  59.3 0.0 copy-start
  59.3 0.0 copy-start.1
  59.3 4.0 %copy.14 = f32[12,8,64,128]{3,2,1,0:T(8,128)} copy(f32[12,8,64,128]{3,2,1,0:T(8,128)} %bitcast.7) | data formatting | bytes 6291456
  63.3 0.0 copy-done
  63.3 0.7 %copy.15 = f32[2,4,64,128]{3,2,1,0:T(8,128)} copy(f32[2,4,64,128]{3,2,1,0:T(8,128)S(1)} %bitcast.11) | data formatting | bytes 524288
  64.0 0.0 copy-done.1
  64.0 0.7 %copy.16 = f32[4,64,128]{2,1,0:T(8,128)} copy(f32[4,64,128]{2,1,0:T(8,128)S(1)} %bitcast.13) | data formatting | bytes 262144
  (10 shorter events, 0.0 us)
Async XLA Ops:
  59.3 4.0 %copy-start = (f32[2,256,128]{2,1,0:T(8,128)S(1)}, f32[2,256,128]{2,1,0:T(8,128)}, u32[]{:S(2)}) copy-start(f32[2,256,128]{2,1,0:T(8,128)} %get-tuple-element.7) | copy-start | bytes 786436
  59.3 4.7 %copy-start.1 = (f32[256,128]{1,0:T(8,128)S(1)}, f32[256,128]{1,0:T(8,128)}, u32[]{:S(2)}) copy-start(f32[256,128]{1,0:T(8,128)} %get-tuple-element.8) | copy-start | bytes 393220
